TPU v7x, 32 devices: a whole 2x2x4 slice. The times are simulated.
32 devices in a mesh: paths: 4 (over y, core), factors: 8 (over z, x).
Axes of the slice: x: 2, y: 2, z: 4, core: 2. Of those that a mesh axis runs over, the one named last changes fastest.
Arguments:
- x_start: float32 [512, 2048], P('factors', 'paths'), may hold values from -3 to 3
- shocks: float32 [4, 512, 2048], P(None, 'factors', 'paths'), may hold values from -6 to 6
- cholesky: float32 [512, 512], P(None, 'factors'), as said below
- reversion: float32 [512], P('factors'), may hold values from 0.05 to 2
- sabr_alpha: float32 [64], replicated, may hold values from 0.2 to 0.6
- sabr_rho: float32 [64], replicated, may hold values from -0.7 to 0.7
- sabr_nu: float32 [64], replicated, may hold values from 0.3 to 1.5
- factor_slice: int32 [512], P('factors'), may hold values from 0 to 63
- notional: float32 [32768], P('factors'), may hold values from -1 to 1
- strike: float32 [32768], P('factors'), may hold values from -3 to 3
- trade_set: int32 [32768], P('factors'), may hold values from 0 to 255
- trade_factor: int32 [32768], P('factors'), may hold values from 0 to 511, as said below
- loss_given: float32 [256], replicated, may hold values from 0.2 to 0.8
Outputs:
- path_adjoint: float32 [512, 2048], P('factors', 'paths')
- sabr_grad: float32 [3, 64], replicated
Inputs may be any that keep to these rules, and one draw needn't show every extreme that they name: `cholesky`: lower triangular with a positive diagonal and rows of unit length. `trade_factor`: trade t's factor lies in [(t // 4096) * 64, (t // 4096 + 1) * 64).
All inputs are finite; a program needn't handle non-finite values.
Results may differ from a plain program's by a relative error of at most 0.004.
Values may be sent and summed in bfloat16 or wider, within the bound.
A program may use at most 192 MiB of HBM per device.

v0:
```python
import math
import jax
import jax.numpy as jnp
from jax import lax
from jax.sharding import PartitionSpec as P

TIME_STEP = 0.25
ROOT_STEP = 0.5
DISCOUNT_RATE = 0.03
PRECISE = lax.Precision.HIGHEST
CONTRACT_FIRST = (((0,), (0,)), ((), ()))


def shortened(value):
    return jax.tree.map(lambda a: a.astype(jnp.bfloat16) if a.dtype == jnp.float32 else a, value)


def smile_terms(squashed, alpha_rows, rho_rows, nu_rows):
    curve = (2.0 - 3.0 * rho_rows * rho_rows) * nu_rows * nu_rows / 24.0
    base = 1.0 + 0.5 * rho_rows * nu_rows * squashed + curve * squashed * squashed
    rho_slope = alpha_rows * (
        0.5 * nu_rows * squashed - 0.25 * rho_rows * nu_rows * nu_rows * squashed * squashed
    )
    nu_slope = alpha_rows * (
        0.5 * rho_rows * squashed
        + (2.0 - 3.0 * rho_rows * rho_rows) * nu_rows * squashed * squashed / 12.0
    )
    level_slope = alpha_rows * (0.5 * rho_rows * nu_rows + 2.0 * curve * squashed)
    return (alpha_rows * base, base, rho_slope, nu_slope, level_slope)


def split_factors(
    x_start,
    shocks,
    cholesky,
    reversion,
    sabr_alpha,
    sabr_rho,
    sabr_nu,
    factor_slice,
    notional,
    strike,
    trade_set,
    trade_factor,
    loss_given,
):
    factor_rows, path_cols = x_start.shape
    step_count = shocks.shape[0]
    total_sets = loss_given.shape[0]
    factor_place = lax.axis_index("factors")
    slice_count = sabr_alpha.shape[0]
    slice_table = (
        factor_slice[:, None] == jnp.arange(slice_count, dtype=jnp.int32)[None, :]
    ).astype(jnp.float32)
    alpha_rows = jnp.dot(slice_table, sabr_alpha, precision=PRECISE)[:, None]
    rho_rows = jnp.dot(slice_table, sabr_rho, precision=PRECISE)[:, None]
    nu_rows = jnp.dot(slice_table, sabr_nu, precision=PRECISE)[:, None]
    local_factor = trade_factor - factor_place * factor_rows
    factor_table = (
        jnp.arange(factor_rows, dtype=jnp.int32)[:, None] == local_factor[None, :]
    ).astype(jnp.float32)
    set_table = (jnp.arange(total_sets, dtype=jnp.int32)[:, None] == trade_set[None, :]).astype(
        jnp.bfloat16
    )
    damping = (1.0 - reversion * TIME_STEP)[:, None]
    state = x_start
    states = [state]
    weights = []
    for step_index in range(step_count):
        squashed = jnp.tanh(state)
        local_vol = smile_terms(squashed, alpha_rows, rho_rows, nu_rows)[0]
        correlate_source = local_vol * shocks[step_index]
        mixed = lax.psum_scatter(
            jnp.dot(cholesky, correlate_source, precision=PRECISE),
            "factors",
            scatter_dimension=0,
            tiled=True,
        )
        state = damping * state + ROOT_STEP * mixed
        states.append(state)
        moneyness = jnp.take(state, local_factor, axis=0) - strike[:, None]
        values = (notional[:, None] * jnp.tanh(moneyness)).astype(jnp.bfloat16)
        discount = math.exp(-DISCOUNT_RATE * TIME_STEP * (step_index + 1))
        partial_sum = jnp.dot(set_table, values, preferred_element_type=jnp.float32)
        exposure = lax.psum(partial_sum.astype(jnp.bfloat16), "factors").astype(jnp.float32)
        weights.append(
            (discount * loss_given[:, None] * jax.nn.sigmoid(exposure)).astype(jnp.bfloat16)
        )
    adjoint = jnp.zeros_like(x_start)
    factor_sums = jnp.zeros((3, factor_rows), jnp.float32)
    for step_index in reversed(range(step_count)):
        moneyness = jnp.take(states[step_index + 1], local_factor, axis=0) - strike[:, None]
        squash_trade = jnp.tanh(moneyness)
        trade_term = (
            notional[:, None]
            * (1.0 - squash_trade * squash_trade)
            * lax.dot_general(
                set_table, weights[step_index], CONTRACT_FIRST, preferred_element_type=jnp.float32
            )
        )
        adjoint = adjoint + jnp.dot(factor_table, trade_term, precision=PRECISE)
        shock_adjoint = jnp.zeros((factor_rows, path_cols), jnp.float32) + lax.dot_general(
            cholesky,
            lax.all_gather(shortened(ROOT_STEP * adjoint), "factors", axis=0, tiled=True),
            CONTRACT_FIRST,
            precision=PRECISE,
        )
        squashed = jnp.tanh(states[step_index])
        local_vol, base, rho_slope, nu_slope, level_slope = smile_terms(
            squashed, alpha_rows, rho_rows, nu_rows
        )
        vol_adjoint = shock_adjoint * shocks[step_index]
        factor_sums = factor_sums + jnp.stack(
            [
                jnp.sum(vol_adjoint * base, axis=1),
                jnp.sum(vol_adjoint * rho_slope, axis=1),
                jnp.sum(vol_adjoint * nu_slope, axis=1),
            ]
        )
        adjoint = damping * adjoint + vol_adjoint * level_slope * (1.0 - squashed * squashed)
    slice_sums = jnp.dot(factor_sums, slice_table, precision=PRECISE)
    return (adjoint, slice_sums)


def per_device(
    x_start,
    shocks,
    cholesky,
    reversion,
    sabr_alpha,
    sabr_rho,
    sabr_nu,
    factor_slice,
    notional,
    strike,
    trade_set,
    trade_factor,
    loss_given,
):
    adjoint, slice_sums = split_factors(
        x_start,
        shocks,
        cholesky,
        reversion,
        sabr_alpha,
        sabr_rho,
        sabr_nu,
        factor_slice,
        notional,
        strike,
        trade_set,
        trade_factor,
        loss_given,
    )
    total_grad = lax.psum(slice_sums, ("paths", "factors"))
    sabr_grad = total_grad / (x_start.shape[1] * lax.axis_size("paths"))
    return (adjoint, sabr_grad)


def solution(mesh):
    return jax.shard_map(
        per_device,
        mesh=mesh,
        in_specs=(
            P("factors", "paths"),
            P(None, "factors", "paths"),
            P(None, "factors"),
            P("factors"),
            P(),
            P(),
            P(),
            P("factors"),
            P("factors"),
            P("factors"),
            P("factors"),
            P("factors"),
            P(),
        ),
        out_specs=(P("factors", "paths"), P()),
        check_vma=False,
    )
```

profile of v0, /device:TPU:0, one launch (start us, length us, event | category | flops | bytes accessed | tf_op | source)
XLA Modules:
  0.0 588.1 jit_solution(14679514657513539477)
XLA Ops:
  10.0 2.1 convolution_bitcast_fusion.3
  14.2 66.8 %reduce-scatter.13.cloned.1.call-done = f32[64,512]{1,0:T(8,128)} async-done(((f32[512,512]{1,0:T(8,128)}), f32[64,512]{1,0:T(8,128)}) %reduce-scatter.13.cloned.1.call-update) | async-done | bytes 131088 | tf_op jit(solution)/shard_map/reduce_scatter | solution.py:73
  85.4 63.6 %reduce-scatter.15.cloned.1.call-done = f32[64,512]{1,0:T(8,128)} async-done(((f32[512,512]{1,0:T(8,128)}), f32[64,512]{1,0:T(8,128)}) %reduce-scatter.15.cloned.1.call-update) | async-done | bytes 131088 | tf_op jit(solution)/shard_map/reduce_scatter | solution.py:73
  152.7 16.8 %gather_fusion.3 = f32[4096,512]{1,0:T(8,128)} fusion(f32[64,512]{1,0:T(8,128)S(1)} %multiply_add_fusion.4, s32[4096]{0:T(1024)S(1)} %fusion.166), kind=kCustom, calls=%fused_computation.3.clone | custom fusion | bytes 16793600 | tf_op jit(solution)/shard_map/jit(_take)/gather | solution.py:92
  169.5 46.4 %reduce-scatter.17.cloned.1.call-done = f32[64,512]{1,0:T(8,128)} async-done(((f32[512,512]{1,0:T(8,128)}), f32[64,512]{1,0:T(8,128)}) %reduce-scatter.17.cloned.1.call-update) | async-done | bytes 131088 | tf_op jit(solution)/shard_map/reduce_scatter | solution.py:73
  219.8 6.3 %fusion.67 = bf16[256,512]{1,0:T(8,128)(2,1)} fusion(f32[4096,512]{1,0:T(8,128)} %gather_fusion.3, f32[4096]{0:T(1024)S(1)} %copy-done.10, f32[4096]{0:T(1024)S(1)} %copy-done.11, pred[4096]{0:T(1024)(128)(4,1)S(1)} %get-tuple-element.32, s32[4096]{0:T(1024)S(1)} %copy-done.3), kind=kOutput, calls=%fused_computation.80 | convolution fusion | flops 1083310080 | bytes 8704000 | tf_op jit(solution)/shard_map/dot_general | solution.py:84
  226.1 16.8 %gather_fusion.2 = f32[4096,512]{1,0:T(8,128)} fusion(f32[64,512]{1,0:T(8,128)S(1)} %multiply_add_fusion.3, s32[4096]{0:T(1024)S(1)} %fusion.166), kind=kCustom, calls=%fused_computation.2.clone | custom fusion | bytes 16793600 | tf_op jit(solution)/shard_map/jit(_take)/gather | solution.py:92
  242.9 6.3 %fusion.66 = bf16[256,512]{1,0:T(8,128)(2,1)} fusion(f32[4096,512]{1,0:T(8,128)} %gather_fusion.2, f32[4096]{0:T(1024)S(1)} %copy-done.10, f32[4096]{0:T(1024)S(1)} %copy-done.11, pred[4096]{0:T(1024)(128)(4,1)S(1)} %get-tuple-element.32, s32[4096]{0:T(1024)S(1)} %copy-done.3), kind=kOutput, calls=%fused_computation.79 | convolution fusion | flops 1083310080 | bytes 8704000 | tf_op jit(solution)/shard_map/dot_general | solution.py:84
  249.2 16.8 %gather_fusion.1 = f32[4096,512]{1,0:T(8,128)} fusion(f32[64,512]{1,0:T(8,128)S(1)} %multiply_add_fusion.2, s32[4096]{0:T(1024)S(1)} %fusion.166), kind=kCustom, calls=%fused_computation.1.clone | custom fusion | bytes 16793600 | tf_op jit(solution)/shard_map/jit(_take)/gather | solution.py:92
  266.0 6.4 %fusion.65 = bf16[256,512]{1,0:T(8,128)(2,1)} fusion(f32[4096,512]{1,0:T(8,128)} %gather_fusion.1, f32[4096]{0:T(1024)S(1)} %copy-done.10, f32[4096]{0:T(1024)S(1)} %copy-done.11, pred[4096]{0:T(1024)(128)(4,1)S(1)} %get-tuple-element.32, s32[4096]{0:T(1024)S(1)} %copy-done.3), kind=kOutput, calls=%fused_computation.78 | convolution fusion | flops 1083310080 | bytes 8704000 | tf_op jit(solution)/shard_map/dot_general | solution.py:84
  272.3 10.4 %reduce-scatter.19.cloned.1.call-done = f32[64,512]{1,0:T(8,128)} async-done(((f32[512,512]{1,0:T(8,128)}), f32[64,512]{1,0:T(8,128)}) %reduce-scatter.19.cloned.1.call-update) | async-done | bytes 131088 | tf_op jit(solution)/shard_map/reduce_scatter | solution.py:73
  283.7 16.8 %gather_fusion = f32[4096,512]{1,0:T(8,128)} fusion(f32[64,512]{1,0:T(8,128)S(1)} %multiply_add_fusion.1, s32[4096]{0:T(1024)S(1)} %fusion.166), kind=kCustom, calls=%fused_computation.clone | custom fusion | bytes 16793600 | tf_op jit(solution)/shard_map/jit(_take)/gather | solution.py:92
  300.5 6.3 %fusion.64 = bf16[256,512]{1,0:T(8,128)(2,1)} fusion(f32[4096,512]{1,0:T(8,128)} %gather_fusion, f32[4096]{0:T(1024)S(1)} %copy-done.10, f32[4096]{0:T(1024)S(1)} %copy-done.11, pred[4096]{0:T(1024)(128)(4,1)S(1)} %get-tuple-element.32, s32[4096]{0:T(1024)S(1)} %copy-done.3), kind=kOutput, calls=%fused_computation.77 | convolution fusion | flops 1083310080 | bytes 8704000 | tf_op jit(solution)/shard_map/dot_general | solution.py:84
  306.9 77.6 %all-reduce.3.cloned.1.call-done = (bf16[256,512]{1,0:T(8,128)(2,1)}, bf16[256,512]{1,0:T(8,128)(2,1)}, bf16[256,512]{1,0:T(8,128)(2,1)}, bf16[256,512]{1,0:T(8,128)(2,1)}) async-done(((bf16[256,512]{1,0:T(8,128)(2,1)}, bf16[256,512]{1,0:T(8,128)(2,1)}, bf16[256,512]{1,0:T(8,128)(2,1)}, bf16[256,512]{1,0:T(8,128)(2,1)}), (bf16[256,512]{1,0:T(8,128)(2,1)}, bf16[256,512]{1,0:T(8,128)(2,1)}, ...) | async-done | bytes 1048592 | tf_op jit(solution)/shard_map/psum | solution.py:85
  384.5 2.5 fusion.38
  387.9 5.4 multiply_convert_fusion.27
  393.3 31.8 %all_gather.12 = bf16[512,512]{1,0:T(8,128)(2,1)S(1)} all-gather(bf16[64,512]{1,0:T(8,128)(2,1)S(1)} %get-tuple-element.45), channel_id=1, replica_groups=mesh['paths'=4,'factors'=8] {'factors'}, dimensions={0}, use_global_device_ids=true | all-gather | bytes 589824 | tf_op jit(solution)/shard_map/all_gather | solution.py:104
  427.0 5.4 multiply_convert_fusion.26
  432.3 31.6 %all_gather.13 = bf16[512,512]{1,0:T(8,128)(2,1)S(1)} all-gather(bf16[64,512]{1,0:T(8,128)(2,1)S(1)} %get-tuple-element.47), channel_id=1, replica_groups=mesh['paths'=4,'factors'=8] {'factors'}, dimensions={0}, use_global_device_ids=true | all-gather | bytes 589824 | tf_op jit(solution)/shard_map/all_gather | solution.py:104
  465.8 5.4 multiply_convert_fusion.25
  471.2 31.5 %all_gather.14 = bf16[512,512]{1,0:T(8,128)(2,1)S(1)} all-gather(bf16[64,512]{1,0:T(8,128)(2,1)S(1)} %get-tuple-element.49), channel_id=1, replica_groups=mesh['paths'=4,'factors'=8] {'factors'}, dimensions={0}, use_global_device_ids=true | all-gather | bytes 589824 | tf_op jit(solution)/shard_map/all_gather | solution.py:104
  504.5 5.4 multiply_convert_fusion.24
  509.9 31.2 %all_gather.15 = bf16[512,512]{1,0:T(8,128)(2,1)S(1)} all-gather(bf16[64,512]{1,0:T(8,128)(2,1)S(1)} %get-tuple-element.51), channel_id=1, replica_groups=mesh['paths'=4,'factors'=8] {'factors'}, dimensions={0}, use_global_device_ids=true | all-gather | bytes 589824 | tf_op jit(solution)/shard_map/all_gather | solution.py:104
  542.9 37.8 %psum.39 = f32[3,64]{1,0:T(4,128)S(1)} all-reduce(f32[3,64]{1,0:T(4,128)S(1)} %fusion.161), channel_id=1, replica_groups=mesh['paths'=4,'factors'=8] {'paths','factors'}, use_global_device_ids=true, to_apply=%region_20.22 | all-reduce | flops 192 | bytes 1536 | tf_op jit(solution)/shard_map/psum | solution.py:155
  (79 shorter events, 26.5 us)
Async XLA Ops:
  7.2 2.8 copy-start
  7.2 142.8 %copy-start.2 = (f32[4,64,512]{2,1,0:T(8,128)S(1)}, f32[4,64,512]{2,1,0:T(8,128)}, u32[]{:S(2)}) copy-start(f32[4,64,512]{2,1,0:T(8,128)} %param.16) | copy-start | bytes 1572868
  7.2 145.4 %copy-start.8 = (s32[4096]{0:T(1024)S(1)}, s32[4096]{0:T(1024)}, u32[]{:S(2)}) copy-start(s32[4096]{0:T(1024)} %param.26) | copy-start | bytes 49156
  7.2 73.7 %reduce-scatter.13.cloned.1.call-start = ((), (), s32[]{:S(2)}) async-start(), calls=%async_computation.4 | async-start | bytes 1179648 | tf_op jit(solution)/shard_map/reduce_scatter | solution.py:73
  13.5 135.6 %reduce-scatter.15.cloned.1.call-start = ((), (), s32[]{:S(2)}) async-start(), calls=%async_computation.5 | async-start | bytes 1179648 | tf_op jit(solution)/shard_map/reduce_scatter | solution.py:73
  85.4 130.5 %reduce-scatter.17.cloned.1.call-start = ((), (), s32[]{:S(2)}) async-start(), calls=%async_computation.6 | async-start | bytes 1179648 | tf_op jit(solution)/shard_map/reduce_scatter | solution.py:73
  152.6 130.2 %reduce-scatter.19.cloned.1.call-start = ((), (), s32[]{:S(2)}) async-start(), calls=%async_computation.7 | async-start | bytes 1179648 | tf_op jit(solution)/shard_map/reduce_scatter | solution.py:73
  152.7 67.1 %copy-start.3 = (s32[4096]{0:T(1024)S(1)}, s32[4096]{0:T(1024)}, u32[]{:S(2)}) copy-start(s32[4096]{0:T(1024)} %param.25) | copy-start | bytes 49156
  152.7 67.1 %copy-start.10 = (f32[4096]{0:T(1024)S(1)}, f32[4096]{0:T(1024)}, u32[]{:S(2)}) copy-start(f32[4096]{0:T(1024)} %param.24) | copy-start | bytes 49156
  152.7 67.1 %copy-start.11 = (f32[4096]{0:T(1024)S(1)}, f32[4096]{0:T(1024)}, u32[]{:S(2)}) copy-start(f32[4096]{0:T(1024)} %param.23) | copy-start | bytes 49156
  219.4 165.1 %all-reduce.3.cloned.1.call-start = ((), (), s32[]{:S(2)}) async-start(), calls=%async_computation.8 | async-start | bytes 2097152 | tf_op jit(solution)/shard_map/psum | solution.py:85
  300.5 6.4 %copy-start.9 = (f32[256]{0:T(256)S(1)}, f32[256]{0:T(256)}, u32[]{:S(2)}) copy-start(f32[256]{0:T(256)} %param.27) | copy-start | bytes 3076
  384.5 3.5 copy-start.1
  384.5 42.4 %slice-start.4 = ((s8[8388608]{0:T(1024)(128)(4,1)}), s8[4194304]{0:T(1024)(128)(4,1)S(1)}, s32[]{:S(2)}) async-start(s8[8388608]{0:T(1024)(128)(4,1)} %bitcast.89), calls=%async_computation.13 | async-start | bytes 8388608
  387.9 37.6 %copy-start.7 = (bf16[256,512]{1,0:T(8,128)(2,1)S(1)}, bf16[256,512]{1,0:T(8,128)(2,1)}, u32[]{:S(2)}) copy-start(bf16[256,512]{1,0:T(8,128)(2,1)} %get-tuple-element.28) | copy-start | bytes 786436
  387.9 39.0 %slice-start.5 = ((s8[8388608]{0:T(1024)(128)(4,1)}), s8[4194304]{0:T(1024)(128)(4,1)S(1)}, s32[]{:S(2)}) async-start(s8[8388608]{0:T(1024)(128)(4,1)} %bitcast.89), calls=%async_computation.14 | async-start | bytes 8388608
  426.9 38.8 %slice-start.2 = ((s8[8388608]{0:T(1024)(128)(4,1)}), s8[4194304]{0:T(1024)(128)(4,1)S(1)}, s32[]{:S(2)}) async-start(s8[8388608]{0:T(1024)(128)(4,1)} %bitcast.87), calls=%async_computation.11 | async-start | bytes 8388608
  427.0 37.4 %copy-start.6 = (bf16[256,512]{1,0:T(8,128)(2,1)S(1)}, bf16[256,512]{1,0:T(8,128)(2,1)}, u32[]{:S(2)}) copy-start(bf16[256,512]{1,0:T(8,128)(2,1)} %get-tuple-element.27) | copy-start | bytes 786436
  427.0 38.8 %slice-start.3 = ((s8[8388608]{0:T(1024)(128)(4,1)}), s8[4194304]{0:T(1024)(128)(4,1)S(1)}, s32[]{:S(2)}) async-start(s8[8388608]{0:T(1024)(128)(4,1)} %bitcast.87), calls=%async_computation.12 | async-start | bytes 8388608
  465.7 38.7 %slice-start = ((s8[8388608]{0:T(1024)(128)(4,1)}), s8[4194304]{0:T(1024)(128)(4,1)S(1)}, s32[]{:S(2)}) async-start(s8[8388608]{0:T(1024)(128)(4,1)} %bitcast.85), calls=%async_computation.9 | async-start | bytes 8388608
  465.8 37.3 %copy-start.5 = (bf16[256,512]{1,0:T(8,128)(2,1)S(1)}, bf16[256,512]{1,0:T(8,128)(2,1)}, u32[]{:S(2)}) copy-start(bf16[256,512]{1,0:T(8,128)(2,1)} %get-tuple-element.26) | copy-start | bytes 786436
  465.8 38.7 %slice-start.1 = ((s8[8388608]{0:T(1024)(128)(4,1)}), s8[4194304]{0:T(1024)(128)(4,1)S(1)}, s32[]{:S(2)}) async-start(s8[8388608]{0:T(1024)(128)(4,1)} %bitcast.85), calls=%async_computation.10 | async-start | bytes 8388608
  504.5 36.6 %copy-start.4 = (f32[64,512]{1,0:T(8,128)S(1)}, f32[64,512]{1,0:T(8,128)}, u32[]{:S(2)}) copy-start(f32[64,512]{1,0:T(8,128)} %param.15) | copy-start | bytes 393220
  504.5 38.2 %copy-start.12 = (s32[64]{0:T(128)S(1)}, s32[64]{0:T(128)}, u32[]{:S(2)}) copy-start(s32[64]{0:T(128)} %param.22) | copy-start | bytes 772
Sparse Core Ops, SparseCore 0:
  13.6 67.3 reduce-scatter.12
  85.5 63.4 reduce-scatter.14
  152.7 63.1 reduce-scatter.16
  219.5 63.1 reduce-scatter.18
  307.0 77.4 all-reduce.2
where the time goes:
time: 593 us; the launch traced here: 588 us
  waiting for transfers between devices  265 us (45%)
  blocking collectives  164 us (28%)
  local copies, waits for them, and re-layouts  73.7 us (12%)
  matrix products  65.5 us (11%)
  between operations  14.4 us (2%)
    reduce_scatter x4, waiting for transfers between devices, split_factors(): lax.psum_scatter(jnp.dot(cholesky, correlate_source, precision=PRECISE),...  187 us
    all_gather x4, blocking collectives, split_factors(): lax.all_gather(shortened(ROOT_STEP * adjoint), 'factors', axis=0, tiled=T...  126 us
    psum x1, waiting for transfers between devices, split_factors(): lax.psum(partial_sum.astype(jnp.bfloat16), 'factors').astype(jnp.float32)  77.6 us
    gather x4, local copies, waits for them, and re-layouts, split_factors(): jnp.take(states[step_index + 1], local_factor, axis=0) - strike[:, None]  67.2 us
    psum x1, blocking collectives, per_device(): total_grad = lax.psum(slice_sums, ('paths', 'factors'))  37.8 us
    dot_general x4, matrix products, split_factors(): partial_sum = jnp.dot(set_table, values, preferred_element_type=jnp.float32)  25.3 us
    dot_general x4, matrix products, split_factors(): adjoint = adjoint + jnp.dot(factor_table, trade_term, precision=PRECISE)  21.5 us
  transfers between devices with their start and end apart: 5, of which 5 were waited for; matrix products, arithmetic and copies ran while one was open for 12% of the time, Pallas kernels for 0%

commit v1 on v0

--- a/solution.py
+++ b/solution.py
@@ -99,9 +99,24 @@
             )
         )
         adjoint = adjoint + jnp.dot(factor_table, trade_term, precision=PRECISE)
+
+        def save_body_on(vals, ndim_at):
+            net_axis = "factors"
+            arr_next, current_value = (lax.axis_size(net_axis), lax.axis_index(net_axis))
+            reached, back = (vals, 1)
+            while back < arr_next:
+                formed = lax.ppermute(
+                    reached, net_axis, [(ii, ii ^ back) for ii in range(arr_next)]
+                )
+                opened = jnp.concatenate([reached, formed], ndim_at)
+                g_now = jnp.concatenate([formed, reached], ndim_at)
+                reached = jnp.where(current_value & back == 0, opened, g_now)
+                back = 2 * back
+            return reached
+
         shock_adjoint = jnp.zeros((factor_rows, path_cols), jnp.float32) + lax.dot_general(
             cholesky,
-            lax.all_gather(shortened(ROOT_STEP * adjoint), "factors", axis=0, tiled=True),
+            save_body_on(shortened(ROOT_STEP * adjoint), 0),
             CONTRACT_FIRST,
             precision=PRECISE,
         )

time: 593 us -> 555 us (0.936)
  blocking collectives: 164 us -> 38.4 us
  waiting for transfers between devices: 265 us -> 333 us
  starting transfers between devices: 0.5 us -> 10.5 us
  matrix products: 65.5 us -> 72.1 us
    all_gather x4 -> x0, blocking collectives: 126 us -> none  [split_factors(): lax.all_gather(shortened(ROOT_STEP * adjoint), 'factors', axis=0, tiled=T...]
    ppermute x0 -> x12, waiting for transfers between devices: none -> 68.3 us  [save_body_on(): lax.ppermute(reached, net_axis, [(ii, ii ^ back) for ii in range(arr_next)])]
    ppermute x0 -> x12, starting transfers between devices: none -> 10.3 us  [save_body_on(): lax.ppermute(reached, net_axis, [(ii, ii ^ back) for ii in range(arr_next)])]
    dot_general x4, matrix products: 21.5 us -> 27.4 us  [split_factors(): adjoint = adjoint + jnp.dot(factor_table, trade_term, precision=PRECISE)]
  transfers between devices with their start and end apart: 5 -> 17, of which waited for: 5 -> 17; matrix products, arithmetic and copies ran while one was open for 12% -> 14% of each run, Pallas kernels for 0% -> 0%
where the time goes in v1:
time: 555 us; the launch traced here: 547 us
  waiting for transfers between devices  333 us (60%)
  local copies, waits for them, and re-layouts  73.5 us (13%)
  matrix products  72.1 us (13%)
  blocking collectives  38.4 us (7%)
  between operations  14.4 us (3%)
  starting transfers between devices  10.5 us (2%)
  other arithmetic  5.61 us (1%)
    reduce_scatter x4, waiting for transfers between devices, split_factors(): lax.psum_scatter(jnp.dot(cholesky, correlate_source, precision=PRECISE),...  187 us
    psum x1, waiting for transfers between devices, split_factors(): lax.psum(partial_sum.astype(jnp.bfloat16), 'factors').astype(jnp.float32)  77.5 us
    ppermute x12, waiting for transfers between devices, save_body_on(): lax.ppermute(reached, net_axis, [(ii, ii ^ back) for ii in range(arr_next)])  68.3 us
    gather x4, local copies, waits for them, and re-layouts, split_factors(): jnp.take(states[step_index + 1], local_factor, axis=0) - strike[:, None]  67.1 us
    psum x1, blocking collectives, per_device(): total_grad = lax.psum(slice_sums, ('paths', 'factors'))  38.4 us
    dot_general x4, matrix products, split_factors(): adjoint = adjoint + jnp.dot(factor_table, trade_term, precision=PRECISE)  27.4 us
    dot_general x4, matrix products, split_factors(): partial_sum = jnp.dot(set_table, values, preferred_element_type=jnp.float32)  25.8 us
  transfers between devices with their start and end apart: 17, of which 17 were waited for; matrix products, arithmetic and copies ran while one was open for 14% of the time, Pallas kernels for 0%

profile of v1, /device:TPU:0, one launch (start us, length us, event | category | flops | bytes accessed | tf_op | source)
XLA Modules:
  0.0 547.0 jit_solution(869553075853794082)
XLA Ops:
  14.1 66.4 %reduce-scatter.13.cloned.1.call-done = f32[64,512]{1,0:T(8,128)} async-done(((f32[512,512]{1,0:T(8,128)}), f32[64,512]{1,0:T(8,128)}) %reduce-scatter.13.cloned.1.call-update) | async-done | bytes 131088 | tf_op jit(solution)/shard_map/reduce_scatter | solution.py:73
  85.0 63.2 %reduce-scatter.15.cloned.1.call-done = f32[64,512]{1,0:T(8,128)} async-done(((f32[512,512]{1,0:T(8,128)}), f32[64,512]{1,0:T(8,128)}) %reduce-scatter.15.cloned.1.call-update) | async-done | bytes 131088 | tf_op jit(solution)/shard_map/reduce_scatter | solution.py:73
  151.9 16.8 %gather_fusion.3 = f32[4096,512]{1,0:T(8,128)} fusion(f32[64,512]{1,0:T(8,128)S(1)} %multiply_add_fusion.4, s32[4096]{0:T(1024)S(1)} %fusion.190), kind=kCustom, calls=%fused_computation.3.clone | custom fusion | bytes 16793600 | tf_op jit(solution)/shard_map/jit(_take)/gather | solution.py:92
  168.7 46.4 %reduce-scatter.17.cloned.1.call-done = f32[64,512]{1,0:T(8,128)} async-done(((f32[512,512]{1,0:T(8,128)}), f32[64,512]{1,0:T(8,128)}) %reduce-scatter.17.cloned.1.call-update) | async-done | bytes 131088 | tf_op jit(solution)/shard_map/reduce_scatter | solution.py:73
  218.7 6.3 %fusion.67 = bf16[256,512]{1,0:T(8,128)(2,1)} fusion(f32[4096,512]{1,0:T(8,128)} %gather_fusion.3, f32[4096]{0:T(1024)S(1)} %copy-done.10, f32[4096]{0:T(1024)S(1)} %copy-done.11, pred[4096]{0:T(1024)(128)(4,1)S(1)} %get-tuple-element.32, s32[4096]{0:T(1024)S(1)} %copy-done.2), kind=kOutput, calls=%fused_computation.80 | convolution fusion | flops 1083310080 | bytes 8704000 | tf_op jit(solution)/shard_map/dot_general | solution.py:84
  225.0 16.8 %gather_fusion.2 = f32[4096,512]{1,0:T(8,128)} fusion(f32[64,512]{1,0:T(8,128)S(1)} %multiply_add_fusion.3, s32[4096]{0:T(1024)S(1)} %fusion.190), kind=kCustom, calls=%fused_computation.2.clone | custom fusion | bytes 16793600 | tf_op jit(solution)/shard_map/jit(_take)/gather | solution.py:92
  241.8 6.3 %fusion.66 = bf16[256,512]{1,0:T(8,128)(2,1)} fusion(f32[4096,512]{1,0:T(8,128)} %gather_fusion.2, f32[4096]{0:T(1024)S(1)} %copy-done.10, f32[4096]{0:T(1024)S(1)} %copy-done.11, pred[4096]{0:T(1024)(128)(4,1)S(1)} %get-tuple-element.32, s32[4096]{0:T(1024)S(1)} %copy-done.2), kind=kOutput, calls=%fused_computation.79 | convolution fusion | flops 1083310080 | bytes 8704000 | tf_op jit(solution)/shard_map/dot_general | solution.py:84
  248.1 16.8 %gather_fusion.1 = f32[4096,512]{1,0:T(8,128)} fusion(f32[64,512]{1,0:T(8,128)S(1)} %multiply_add_fusion.2, s32[4096]{0:T(1024)S(1)} %fusion.190), kind=kCustom, calls=%fused_computation.1.clone | custom fusion | bytes 16793600 | tf_op jit(solution)/shard_map/jit(_take)/gather | solution.py:92
  264.9 6.4 %fusion.65 = bf16[256,512]{1,0:T(8,128)(2,1)} fusion(f32[4096,512]{1,0:T(8,128)} %gather_fusion.1, f32[4096]{0:T(1024)S(1)} %copy-done.10, f32[4096]{0:T(1024)S(1)} %copy-done.11, pred[4096]{0:T(1024)(128)(4,1)S(1)} %get-tuple-element.32, s32[4096]{0:T(1024)S(1)} %copy-done.2), kind=kOutput, calls=%fused_computation.78 | convolution fusion | flops 1083310080 | bytes 8704000 | tf_op jit(solution)/shard_map/dot_general | solution.py:84
  271.3 10.6 %reduce-scatter.19.cloned.1.call-done = f32[64,512]{1,0:T(8,128)} async-done(((f32[512,512]{1,0:T(8,128)}), f32[64,512]{1,0:T(8,128)}) %reduce-scatter.19.cloned.1.call-update) | async-done | bytes 131088 | tf_op jit(solution)/shard_map/reduce_scatter | solution.py:73
  282.8 16.8 %gather_fusion = f32[4096,512]{1,0:T(8,128)} fusion(f32[64,512]{1,0:T(8,128)S(1)} %multiply_add_fusion.1, s32[4096]{0:T(1024)S(1)} %fusion.190), kind=kCustom, calls=%fused_computation.clone | custom fusion | bytes 16793600 | tf_op jit(solution)/shard_map/jit(_take)/gather | solution.py:92
  299.6 6.8 %fusion.64 = bf16[256,512]{1,0:T(8,128)(2,1)} fusion(f32[4096,512]{1,0:T(8,128)} %gather_fusion, f32[4096]{0:T(1024)S(1)} %copy-done.10, f32[4096]{0:T(1024)S(1)} %copy-done.11, pred[4096]{0:T(1024)(128)(4,1)S(1)} %get-tuple-element.32, s32[4096]{0:T(1024)S(1)} %copy-done.2), kind=kOutput, calls=%fused_computation.77 | convolution fusion | flops 1083310080 | bytes 8704000 | tf_op jit(solution)/shard_map/dot_general | solution.py:84
  306.4 77.5 %all-reduce.3.cloned.1.call-done = (bf16[256,512]{1,0:T(8,128)(2,1)}, bf16[256,512]{1,0:T(8,128)(2,1)}, bf16[256,512]{1,0:T(8,128)(2,1)}, bf16[256,512]{1,0:T(8,128)(2,1)}) async-done(((bf16[256,512]{1,0:T(8,128)(2,1)}, bf16[256,512]{1,0:T(8,128)(2,1)}, bf16[256,512]{1,0:T(8,128)(2,1)}, bf16[256,512]{1,0:T(8,128)(2,1)}), (bf16[256,512]{1,0:T(8,128)(2,1)}, bf16[256,512]{1,0:T(8,128)(2,1)}, ...) | async-done | bytes 1048592 | tf_op jit(solution)/shard_map/psum | solution.py:85
  387.4 5.4 multiply_convert_fusion.27
  405.0 9.0 %collective-permute-done.2 = bf16[256,512]{1,0:T(8,128)(2,1)S(1)} collective-permute-done((bf16[256,512]{1,0:T(8,128)(2,1)S(1)}, bf16[256,512]{1,0:T(8,128)(2,1)S(1)}, u32[]{:S(2)}, u32[]{:S(2)}) %collective-permute-start.2) | collective-permute-done | bytes 262176 | tf_op jit(solution)/shard_map/ppermute | solution.py:108
  414.4 11.1 %multiply_convert_fusion.26 = (bf16[64,512]{1,0:T(8,128)(2,1)S(1)}, f32[64,512]{1,0:T(8,128)S(1)}) fusion(f32[4096,512]{1,0:T(8,128)S(1)} %fusion.36, f32[4096,512]{1,0:T(8,128)} %gather_fusion.1, f32[4096]{0:T(1024)S(1)} %copy-done.10, f32[4096]{0:T(1024)S(1)} %copy-done.11, pred[4096]{0:T(1024)(128)(4,1)S(1)} %get-tuple-element.32, ...), kind=kOutput, calls=%fused_computation.211 | convolution fusion | flops 1623851008 | bytes 17421312 | tf_op jit(solution)/shard_map/dot_general | solution.py:101
  430.0 5.0 collective-permute-done.4
  436.7 9.7 %collective-permute-done.5 = bf16[256,512]{1,0:T(8,128)(2,1)S(1)} collective-permute-done((bf16[256,512]{1,0:T(8,128)(2,1)S(1)}, bf16[256,512]{1,0:T(8,128)(2,1)S(1)}, u32[]{:S(2)}, u32[]{:S(2)}) %collective-permute-start.5) | collective-permute-done | bytes 262176 | tf_op jit(solution)/shard_map/ppermute | solution.py:108
  446.9 5.4 multiply_convert_fusion.25
  456.7 5.0 collective-permute-done.7
  463.3 9.7 %collective-permute-done.8 = bf16[256,512]{1,0:T(8,128)(2,1)S(1)} collective-permute-done((bf16[256,512]{1,0:T(8,128)(2,1)S(1)}, bf16[256,512]{1,0:T(8,128)(2,1)S(1)}, u32[]{:S(2)}, u32[]{:S(2)}) %collective-permute-start.8) | collective-permute-done | bytes 262176 | tf_op jit(solution)/shard_map/ppermute | solution.py:108
  473.5 5.6 %multiply_convert_fusion.24 = (bf16[64,512]{1,0:T(8,128)(2,1)S(1)}, f32[64,512]{1,0:T(8,128)S(1)}) fusion(f32[4096,512]{1,0:T(8,128)S(1)} %fusion.32, f32[4096,512]{1,0:T(8,128)S(1)} %bitcast.82, f32[4096]{0:T(1024)S(1)} %copy-done.10, f32[4096]{0:T(1024)S(1)} %copy-done.11, pred[4096]{0:T(1024)(128)(4,1)S(1)} %get-tuple-element.32, ...), kind=kOutput, calls=%fused_computation.209 | convolution fusion | flops 1623851008 | bytes 17421312 | tf_op jit(solution)/shard_map/dot_general | solution.py:101
  488.7 10.7 %collective-permute-done.11 = bf16[256,512]{1,0:T(8,128)(2,1)S(1)} collective-permute-done((bf16[256,512]{1,0:T(8,128)(2,1)S(1)}, bf16[256,512]{1,0:T(8,128)(2,1)S(1)}, u32[]{:S(2)}, u32[]{:S(2)}) %collective-permute-start.11) | collective-permute-done | bytes 262176 | tf_op jit(solution)/shard_map/ppermute | solution.py:108
  501.3 38.4 %psum.39 = f32[3,64]{1,0:T(4,128)S(1)} all-reduce(f32[3,64]{1,0:T(4,128)S(1)} %fusion.185), channel_id=1, replica_groups=mesh['paths'=4,'factors'=8] {'paths','factors'}, use_global_device_ids=true, to_apply=%region_20.22 | all-reduce | flops 192 | bytes 1536 | tf_op jit(solution)/shard_map/psum | solution.py:170
  (102 shorter events, 60.7 us)
Async XLA Ops:
  7.2 142.0 %copy-start.3 = (f32[4,64,512]{2,1,0:T(8,128)S(1)}, f32[4,64,512]{2,1,0:T(8,128)}, u32[]{:S(2)}) copy-start(f32[4,64,512]{2,1,0:T(8,128)} %param.16) | copy-start | bytes 1572868
  7.2 144.6 %copy-start.8 = (s32[4096]{0:T(1024)S(1)}, s32[4096]{0:T(1024)}, u32[]{:S(2)}) copy-start(s32[4096]{0:T(1024)} %param.26) | copy-start | bytes 49156
  7.2 73.4 %reduce-scatter.13.cloned.1.call-start = ((), (), s32[]{:S(2)}) async-start(), calls=%async_computation.4 | async-start | bytes 1179648 | tf_op jit(solution)/shard_map/reduce_scatter | solution.py:73
  13.4 134.8 %reduce-scatter.15.cloned.1.call-start = ((), (), s32[]{:S(2)}) async-start(), calls=%async_computation.5 | async-start | bytes 1179648 | tf_op jit(solution)/shard_map/reduce_scatter | solution.py:73
  85.0 130.1 %reduce-scatter.17.cloned.1.call-start = ((), (), s32[]{:S(2)}) async-start(), calls=%async_computation.6 | async-start | bytes 1179648 | tf_op jit(solution)/shard_map/reduce_scatter | solution.py:73
  151.8 130.1 %reduce-scatter.19.cloned.1.call-start = ((), (), s32[]{:S(2)}) async-start(), calls=%async_computation.7 | async-start | bytes 1179648 | tf_op jit(solution)/shard_map/reduce_scatter | solution.py:73
  151.8 66.8 %copy-start.2 = (s32[4096]{0:T(1024)S(1)}, s32[4096]{0:T(1024)}, u32[]{:S(2)}) copy-start(s32[4096]{0:T(1024)} %param.25) | copy-start | bytes 49156
  151.9 66.8 %copy-start.10 = (f32[4096]{0:T(1024)S(1)}, f32[4096]{0:T(1024)}, u32[]{:S(2)}) copy-start(f32[4096]{0:T(1024)} %param.24) | copy-start | bytes 49156
  151.9 66.8 %copy-start.11 = (f32[4096]{0:T(1024)S(1)}, f32[4096]{0:T(1024)}, u32[]{:S(2)}) copy-start(f32[4096]{0:T(1024)} %param.23) | copy-start | bytes 49156
  218.6 165.3 %all-reduce.3.cloned.1.call-start = ((), (), s32[]{:S(2)}) async-start(), calls=%async_computation.8 | async-start | bytes 2097152 | tf_op jit(solution)/shard_map/psum | solution.py:85
  392.8 4.3 collective-permute-start
  397.1 5.0 collective-permute-start.1
  402.2 11.7 %collective-permute-start.2 = (bf16[256,512]{1,0:T(8,128)(2,1)S(1)}, bf16[256,512]{1,0:T(8,128)(2,1)S(1)}, u32[]{:S(2)}, u32[]{:S(2)}) collective-permute-start(bf16[256,512]{1,0:T(8,128)(2,1)S(1)} %maximum_select_fusion.8), channel_id=1, source_target_pairs={{0,4},{1,5},{2,6},{3,7},{4,0},{5,1},{6,2},{7,3},{8,12},{9,13},{10,... | collective-permute-start | bytes 786440 | tf_op jit(solution)/shard_map/ppermute | solution.py:108
  414.4 32.5 %slice-start.2 = ((s8[8388608]{0:T(1024)(128)(4,1)}), s8[4194304]{0:T(1024)(128)(4,1)S(1)}, s32[]{:S(2)}) async-start(s8[8388608]{0:T(1024)(128)(4,1)} %bitcast.83), calls=%async_computation.11 | async-start | bytes 8388608
  414.4 32.5 %slice-start.3 = ((s8[8388608]{0:T(1024)(128)(4,1)}), s8[4194304]{0:T(1024)(128)(4,1)S(1)}, s32[]{:S(2)}) async-start(s8[8388608]{0:T(1024)(128)(4,1)} %bitcast.83), calls=%async_computation.12 | async-start | bytes 8388608
  425.5 4.3 collective-permute-start.3
  429.9 5.0 collective-permute-start.4
  435.0 11.4 %collective-permute-start.5 = (bf16[256,512]{1,0:T(8,128)(2,1)S(1)}, bf16[256,512]{1,0:T(8,128)(2,1)S(1)}, u32[]{:S(2)}, u32[]{:S(2)}) collective-permute-start(bf16[256,512]{1,0:T(8,128)(2,1)S(1)} %maximum_select_fusion.9), channel_id=1, source_target_pairs={{0,4},{1,5},{2,6},{3,7},{4,0},{5,1},{6,2},{7,3},{8,12},{9,13},{10,... | collective-permute-start | bytes 786440 | tf_op jit(solution)/shard_map/ppermute | solution.py:108
  452.3 4.3 collective-permute-start.6
  456.7 5.0 collective-permute-start.7
  461.8 11.3 %collective-permute-start.8 = (bf16[256,512]{1,0:T(8,128)(2,1)S(1)}, bf16[256,512]{1,0:T(8,128)(2,1)S(1)}, u32[]{:S(2)}, u32[]{:S(2)}) collective-permute-start(bf16[256,512]{1,0:T(8,128)(2,1)S(1)} %maximum_select_fusion.10), channel_id=1, source_target_pairs={{0,4},{1,5},{2,6},{3,7},{4,0},{5,1},{6,2},{7,3},{8,12},{9,13},{10,... | collective-permute-start | bytes 786440 | tf_op jit(solution)/shard_map/ppermute | solution.py:108
  479.1 4.3 collective-permute-start.9
  483.5 5.0 collective-permute-start.10
  488.6 10.9 %collective-permute-start.11 = (bf16[256,512]{1,0:T(8,128)(2,1)S(1)}, bf16[256,512]{1,0:T(8,128)(2,1)S(1)}, u32[]{:S(2)}, u32[]{:S(2)}) collective-permute-start(bf16[256,512]{1,0:T(8,128)(2,1)S(1)} %maximum_select_fusion.11), channel_id=1, source_target_pairs={{0,4},{1,5},{2,6},{3,7},{4,0},{5,1},{6,2},{7,3},{8,12},{9,13},{10,... | collective-permute-start | bytes 786440 | tf_op jit(solution)/shard_map/ppermute | solution.py:108
  (10 other events, 171.9 us)
Sparse Core Ops, SparseCore 0:
  13.6 66.9 reduce-scatter.12
  85.1 63.0 reduce-scatter.14
  151.9 63.1 reduce-scatter.16
  218.7 63.0 reduce-scatter.18
  306.5 77.3 all-reduce.2
